TPU v7x, 256 devices: a whole 4x4x8 slice. The times are simulated.
256 devices in a mesh: depth: 8 (over z_lo, core), tile: 32 (over y, x, z_hi).
Axes of the slice: x: 4, y: 4, z: 8 (z_hi: 2, z_lo: 4; z = z_hi * 4 + z_lo), core: 2. Of those that a mesh axis runs over, the one named last changes fastest.
Arguments:
- volume: float32 [32, 1024, 1024], P('depth', 'tile'), may hold values from -6 to 6
- measured: float32 [3, 1024, 1024], P(None, 'tile'), may hold values from -12 to 12
- row_bank: float32 [256, 2, 33], replicated, may hold values from -0.5 to 0.5
- col_bank: float32 [256, 2, 33], replicated, may hold values from -0.5 to 0.5
- kernel_index: int32 [169, 32], P(None, 'depth'), may hold values from 0 to 255
- view_order: int32 [3], replicated, may hold values from 0 to 168
Outputs:
- volume_out: float32 [32, 1024, 1024], P('depth', 'tile')
- last_residual: float32 [1024, 1024], P('tile')
All inputs are finite; a program needn't handle non-finite values.
Results may differ from a plain program's by a relative error of at most 0.00013.
Values sent between devices are 32-bit elements; how exact they have to be, the bound alone decides.
A program may use at most 64 MiB of HBM per device.

v0:
```python
import functools

import jax
import jax.numpy as jnp
from jax import lax
from jax.experimental import pallas as pl
from jax.experimental.pallas import tpu as pltpu
from jax.sharding import PartitionSpec as P

MESH = pl.DeviceIdType.MESH
DESCENT = 0.5
SHRINK = 0.1
LANES = 128
F32, BF16 = jnp.float32, jnp.bfloat16


def split(x):
    hi = x.astype(BF16)
    return hi, (x - hi.astype(F32)).astype(BF16)


def dot(a, b):
    return jnp.dot(a, b, preferred_element_type=F32)


def lane_of(shape):
    return lax.broadcasted_iota(jnp.int32, shape, len(shape) - 1)


def sheared(row, rows):
    wide = jnp.broadcast_to(row, (rows, row.shape[1]))
    return pltpu.roll(wide, 0, 1, stride=1, stride_axis=0)


def kernel(
    nt, steps,
    vol, meas, rowb, colb, kidx, vord,
    out, resid,
    V, mz, raw, H, TFh, TFl, TB, AF, A2, AP, Wh, Wl, S, XF, rb1, rb2, res, R, RX,
    rs_send, rs1_recv, rs2_recv, ag_send, agx_send, ag_recv, agx_recv,
    loc_sem, pair_send, pair_recv, raw_sem, fin_loc, fin_send, fin_recv,
):
    dd, t = lax.axis_index("depth"), lax.axis_index("tile")
    kap, z = dd % 2, dd // 2
    p, c = t % 2, t // 2
    other = 1 - kap
    partner = (z * 2 + other, t)
    reach = (rowb.shape[0] - 1) // 2
    edge = jnp.logical_or(
        jnp.logical_and(kap == 0, z == 3), jnp.logical_and(kap == 1, z == 0)
    )

    def cols(block):
        return pl.ds(pl.multiple_of(block * LANES, LANES), LANES)

    def send(src, dst, s, r, dev):
        return pltpu.make_async_remote_copy(
            src_ref=src, dst_ref=dst, send_sem=s, recv_sem=r, device_id=dev, device_id_type=MESH
        )

    mine = pl.ds(kap * 4, 4)
    theirs = pl.ds(other * 4, 4)

    def block_of(core, lb):
        return core * 4 + lb if lb < 4 else 4 - core

    loads = [
        pltpu.make_async_copy(vol.at[:, :, cols(block_of(kap, lb))], V.at[lb, mine], loc_sem.at[lb])
        for lb in range(5)
    ]
    loads.append(pltpu.make_async_copy(meas.at[:, :, cols(kap * 4 + z)], mz, loc_sem.at[5]))
    for cp in loads:
        cp.start()
    gives = [
        send(vol.at[:, :, cols(block_of(other, lb))], V.at[lb, mine], pair_send.at[lb], pair_recv.at[lb], partner)
        for lb in range(5)
    ]
    for cp in gives:
        cp.start()
    taps = rowb.shape[0]
    j = lax.broadcasted_iota(jnp.int32, (16, rowb.shape[2]), 0)
    pick = jnp.zeros(j.shape, jnp.int32)
    for k in range(steps):
        view = vord[k]
        for d in range(4):
            pick = jnp.where(j == k * 4 + d, kidx[d, view], pick)
    onehot = (pick == lane_of(j.shape)).astype(F32)
    raw[kap] = jnp.zeros(raw.shape[1:], F32)
    for i, bank in enumerate((rowb, colb)):
        for r in range(2):
            raw[kap, 2 * i + r, :, 0:taps] = lax.dot_general(
                onehot, bank[:, r, :], (((1,), (1,)), ((), ())),
                precision=lax.Precision.HIGHEST, preferred_element_type=F32,
            )
    give_raw = send(raw.at[kap], raw.at[kap], raw_sem.at[0], raw_sem.at[1], partner)
    give_raw.start()
    give_raw.wait()
    q = lax.broadcasted_iota(jnp.int32, (LANES, 640), 0)
    l = lax.broadcasted_iota(jnp.int32, (LANES, 640), 1)
    fwd = jnp.logical_and(l < 256, l == jnp.where(q <= reach, reach - q, 256 + reach - q))
    bwd = jnp.logical_and(
        jnp.logical_and(l >= 256, l < 512), l - 256 == jnp.where(q >= reach, q - reach, 256 + q - reach)
    )
    row = l - 512 == 2 * reach - q
    place = jnp.where(fwd | row, 1.0, jnp.where(bwd, -DESCENT, 0.0)).astype(F32)
    H[...] = jnp.dot(
        raw[...].reshape(-1, LANES), place, precision=lax.Precision.HIGHEST, preferred_element_type=F32
    ).reshape(H.shape)

    lane32 = lane_of((32, LANES))
    low = lane32 < 64
    keep = low == (kap == 0)

    def taps_of(src, j, base, start, stop):
        rows = H[src, j, :, start:stop]
        mine = lax.broadcasted_iota(jnp.int32, rows.shape, 0) == base
        return jnp.sum(jnp.where(mine, rows, 0.0), axis=0, keepdims=True)

    def row_mats(k, d):
        base = k * 4 + d % 4
        for r in range(2):
            m = sheared(taps_of(d // 4, r, base, 512, 640), 32)
            m = jnp.where(jnp.logical_and(t == 0, lane32 < reach), 0.0, m)
            m = jnp.where(jnp.logical_and(t == nt - 1, lane32 >= 3 * reach), 0.0, m)
            yield r, m

    def prep_forward(k):
        def plane(d, carry):
            base = k * 4 + d % 4
            for r in range(2):
                hi, lo = split(sheared(taps_of(d // 4, 2 + r, base, 0, 256), LANES))
                at = slice(r * LANES, (r + 1) * LANES)
                TFh[d, 0:128, at] = hi[:, 0:128]
                TFh[d, 128:256, at] = hi[:, 128:256]
                TFl[d, 0:128, at] = lo[:, 0:128]
                TFl[d, 128:256, at] = lo[:, 128:256]
            for r, m in row_mats(k, d):
                AF[d, r * 32 : (r + 1) * 32, :] = m
            return carry

        lax.fori_loop(0, 8, plane, 0)
        for j in range(4):
            m = AF[2 * j : 2 * j + 2].reshape(LANES, LANES).T[0:64]
            hi, lo = split(m)
            A2[0:64, j * LANES : (j + 1) * LANES] = hi
            A2[64:128, j * LANES : (j + 1) * LANES] = lo

    def prep_backward(k):
        def plane(d, carry):
            base = k * 4 + d % 4
            for r in range(2):
                hi, lo = split(sheared(taps_of(d // 4, 2 + r, base, 256, 512), LANES))
                for e in range(2):
                    at = slice(e * 256 + r * LANES, e * 256 + (r + 1) * LANES)
                    TB[d, at, 0:128] = hi[:, e * 128 : (e + 1) * 128]
                    TB[d, at, 128:256] = lo[:, e * 128 : (e + 1) * 128]
            for r, m in row_mats(k, d):
                hi, lo = split(m)
                at = slice(r * 32, (r + 1) * 32)
                both = jnp.where(low, hi.astype(F32), pltpu.roll(lo.astype(F32), 64, 1))
                AP[d, at, 0:128] = both.astype(BF16)
                AP[d, at, 128:256] = hi
            return carry

        lax.fori_loop(0, 8, plane, 0)

    def forward():
        def plane(d, carry):
            v = [V[lb, d] for lb in range(5)]
            rows = []
            for lb in range(4):
                near = jnp.where(low, v[lb + 1], v[(lb + 4) % 5])
                rows.append(jnp.concatenate([v[lb], near], axis=1))
            hi, lo = split(jnp.concatenate(rows, axis=0))
            w = dot(jnp.concatenate([hi, lo], axis=0), TFh[d])
            w = w[0:128] + w[128:256] + dot(hi, TFl[d])
            hi, lo = split(w)
            for lb in range(4):
                for r in range(2):
                    src = (slice(lb * 32, (lb + 1) * 32), slice(r * 128, (r + 1) * 128))
                    dst = (d, slice(r * 32, (r + 1) * 32), slice(lb * 128, (lb + 1) * 128))
                    Wh[dst] = hi[src]
                    Wl[dst] = lo[src]
            return carry

        lax.fori_loop(0, 8, plane, 0)
        s = dot(A2[...], Wh[...].reshape(512, 512))
        s = s[0:64] + s[64:128] + dot(A2[0:64], Wl[...].reshape(512, 512))
        for lb in range(4):
            S[lb] = s[:, lb * 128 : (lb + 1) * 128]

    def backward(k):
        parts = []
        for lb in range(5):
            if lb < 4:
                r = R[lb]
            else:
                r = jnp.where((lane_of((64, LANES)) < 64) == (kap == 0), RX[k], 0.0)
            hi, lo = split(r)
            parts.append(jnp.concatenate([hi, hi, lo, lo], axis=0))
        XF[...] = dot(AP[...].reshape(512, 256), jnp.concatenate(parts, axis=1)).reshape(8, 64, 640)

        def plane(d, carry):
            x = [[XF[d, r * 32 : (r + 1) * 32, lb * 128 : (lb + 1) * 128] for r in range(2)] for lb in range(5)]
            rows = []
            for lb in range(5):
                near = [jnp.where(low, x[(lb + 1) % 5][r], x[(lb + 4) % 5][r]) for r in range(2)]
                rows.append(jnp.concatenate(x[lb] + near, axis=1))
            hi, lo = split(jnp.concatenate(rows, axis=0))
            g = dot(jnp.concatenate([hi, lo], axis=0), TB[d])
            g = g[0:160, 0:128] + (g[0:160, 128:256] + (g[160:320, 0:128] + g[160:320, 128:256]))
            for lb in range(5):
                moved = V[lb, d] + g[lb * 32 : (lb + 1) * 32]
                new = moved - jnp.clip(moved, -SHRINK, SHRINK)
                new = jnp.where(k == steps - 1, moved, new)
                V[lb, d] = new if lb < 4 else jnp.where(keep, new, 0.0)
            return carry

        lax.fori_loop(0, 8, plane, 0)

    def rs_copies():
        slot = p * 4 + z
        n = 0
        cl = c + p - 1
        for hx in range(2):
            for bo in range(4):
                h, b = (p + hx) % 2, (z + bo) % 4
                if hx or bo:
                    rows = pl.ds(pl.multiple_of(((1 - p) * 2 + h) * 16, 16), 16)
                    yield send(S.at[b, rows], rb1.at[slot], rs_send.at[n], rs1_recv.at[slot], (2 * b + kap, 2 * c + h))
                    n += 1
        for h in range(2):
            for bo in range(4):
                b = (z + bo) % 4
                rows = pl.ds(pl.multiple_of((2 * p + h) * 16, 16), 16)
                tile = (2 * cl + 3 * h + nt) % nt
                yield send(S.at[b, rows], rb2.at[slot], rs_send.at[n], rs2_recv.at[slot], (2 * b + kap, tile))
                n += 1

    def rs_wait():
        for hx in range(2):
            for bo in range(4):
                slot = ((p + hx) % 2) * 4 + (z + bo) % 4
                if hx or bo:
                    send(res.at[0], rb1.at[slot], rs_send.at[0], rs1_recv.at[slot], partner).wait_recv()
                send(res.at[0], rb2.at[slot], rs_send.at[0], rs2_recv.at[slot], partner).wait_recv()

    def ag_copies(k, far):
        n = 0
        core = other if far else kap
        cl = c - p
        for kind in range(2):
            for hx in range(2):
                for bo in range(4):
                    h, b = (p + hx) % 2, (z + bo) % 4
                    if kind == 0:
                        tile, g = 2 * c + h, (1 - h) * 2 + p
                        if not (hx or bo or far):
                            continue
                    else:
                        tile, g = (2 * cl + 2 - h + nt) % nt, 2 * h + p
                    rows = pl.ds(pl.multiple_of(g * 16, 16), 16)
                    dev = (2 * b + core, tile)
                    if far:
                        yield send(res.at[kind], RX.at[k, rows], agx_send.at[n], agx_recv.at[k, g], dev)
                    else:
                        yield send(res.at[kind], R.at[z, rows], ag_send.at[n], ag_recv.at[g, z], dev)
                    n += 1

    def ag_wait(k):
        for g in range(4):
            for b in range(4):
                @pl.when(jnp.logical_or(g != 2 - p, b != z))
                def _():
                    send(res.at[0], R.at[b, g * 16 : g * 16 + 16], ag_send.at[0], ag_recv.at[g, b], partner).wait_recv()
            send(res.at[0], RX.at[k, g * 16 : g * 16 + 16], ag_send.at[0], agx_recv.at[k, g], partner).wait_recv()

    prep_forward(0)
    for cp in loads:
        cp.wait()
    for cp in gives:
        cp.wait()
    for d in range(8):
        V[4, d] = jnp.where(keep, V[4, d], 0.0)

    def step(k, carry):
        forward()
        S[z, 16:48] = S[z, 16:48] - mz[k]
        for cp in rs_copies():
            cp.start()
        prep_backward(k)
        rs_wait()
        own = pl.ds(pl.multiple_of((2 - p) * 16, 16), 16)
        total1 = S[z, own]
        total2 = rb2[p * 4 + z]
        for hx in range(2):
            for bo in range(4):
                if hx or bo:
                    slot = ((p + hx) % 2) * 4 + (z + bo) % 4
                    total1 = total1 + rb1[slot]
                    total2 = total2 + rb2[slot]
        res[0] = total1
        res[1] = total2
        for cp in ag_copies(k, False):
            cp.start()

        @pl.when(edge)
        def _():
            for cp in ag_copies(k, True):
                cp.start()

        R[z, own] = total1
        prep_forward(jnp.minimum(k + 1, steps - 1))
        for cp in rs_copies():
            cp.wait_send()
        ag_wait(k)
        backward(k)
        for cp in ag_copies(k, False):
            cp.wait_send()

        @pl.when(edge)
        def _():
            for cp in ag_copies(k, True):
                cp.wait_send()

        return carry

    lax.fori_loop(0, steps, step, 0)

    ends = []
    for lb in range(4):
        here = cols(kap * 4 + lb)
        ends.append(pltpu.make_async_copy(V.at[lb, mine], out.at[:, :, here], fin_loc.at[lb]))
        ends.append(pltpu.make_async_copy(R.at[lb, 16:48], resid.at[:, here], fin_loc.at[4 + lb]))
        ends.append(send(V.at[lb, theirs], out.at[:, :, here], fin_send.at[lb], fin_recv.at[lb], partner))
        ends.append(send(R.at[lb, 16:48], resid.at[:, here], fin_send.at[4 + lb], fin_recv.at[4 + lb], partner))
    for cp in ends:
        cp.start()
    for cp in ends:
        cp.wait()


def solution(mesh):
    nt = mesh.shape["tile"]

    def per_device(volume, measured, row_bank, col_bank, kernel_index, view_order):
        steps, rows, width = measured.shape
        vm, dma = pltpu.VMEM, pltpu.SemaphoreType.DMA
        anywhere = pl.BlockSpec(memory_space=pl.ANY)
        moved, resid = pl.pallas_call(
            functools.partial(kernel, nt, steps),
            name="ista",
            out_shape=(
                jax.ShapeDtypeStruct(volume.shape, F32),
                jax.ShapeDtypeStruct((rows, width), F32),
            ),
            in_specs=[
                anywhere,
                anywhere,
                pl.BlockSpec(memory_space=vm),
                pl.BlockSpec(memory_space=vm),
                pl.BlockSpec(memory_space=pltpu.SMEM),
                pl.BlockSpec(memory_space=pltpu.SMEM),
            ],
            out_specs=(anywhere, anywhere),
            scratch_shapes=[
                vm((5, 8, rows, LANES), F32),
                vm((steps, rows, LANES), F32),
                vm((2, 4, 16, LANES), F32),
                vm((2, 4, 16, 640), F32),
                vm((8, 256, 256), BF16),
                vm((8, 256, 256), BF16),
                vm((8, 512, 256), BF16),
                vm((8, 64, LANES), F32),
                vm((128, 512), BF16),
                vm((8, 64, 256), BF16),
                vm((8, 64, 512), BF16),
                vm((8, 64, 512), BF16),
                vm((4, 64, LANES), F32),
                vm((8, 64, 640), F32),
                vm((8, 16, LANES), F32),
                vm((8, 16, LANES), F32),
                vm((2, 16, LANES), F32),
                vm((4, 64, LANES), F32),
                vm((steps, 64, LANES), F32),
                dma((15,)),
                dma((8,)),
                dma((8,)),
                dma((15,)),
                dma((16,)),
                dma((4, 4)),
                dma((steps, 4)),
                dma((6,)),
                dma((5,)),
                dma((5,)),
                dma((2,)),
                dma((8,)),
                dma((8,)),
                dma((8,)),
            ],
            compiler_params=pltpu.CompilerParams(has_side_effects=True, vmem_limit_bytes=60 * 1024 * 1024),
        )(volume, measured, row_bank.T, col_bank.T, kernel_index.T, view_order)
        return moved - jnp.clip(moved, -SHRINK, SHRINK), resid

    return jax.shard_map(
        per_device,
        mesh=mesh,
        in_specs=(P("depth", "tile", None), P(None, "tile", None), P(), P(), P(None, "depth"), P()),
        out_specs=(P("depth", "tile", None), P("tile", None)),
        check_vma=False,
    )
```

profile of v0, /device:TPU:1, one launch (start us, length us, event | category | flops | bytes accessed | tf_op | source)
XLA Modules:
  0.0 85.4 jit_solution(13571943815329272371)
XLA Ops:
  0.6 82.1 %ista.1 = (f32[4,32,1024]{2,1,0:T(8,128)}, f32[32,1024]{1,0:T(8,128)}) custom-call(f32[4,32,1024]{2,1,0:T(8,128)} %vol.1, f32[3,32,1024]{2,1,0:T(8,128)} %meas.1, f32[33,2,256]{2,1,0:T(2,128)} %bitcast.3, f32[33,2,256]{2,1,0:T(2,128)} %bitcast.4, s32[4,169]{1,0:T(4,128)} %bitcast.5, s32[3]{0:T(128)} %vord.1), custom_call_target="tpu_custom_call" | custom-call | tf_op jit(solution)/shard_map/ista/pallas_call | solution.py:350
  82.8 0.0 copy-start
  82.8 1.9 %clamp_subtract_fusion = f32[4,32,1024]{2,1,0:T(8,128)} fusion(f32[4,32,1024]{2,1,0:T(8,128)} %get-tuple-element.4), kind=kLoop, calls=%fused_computation | loop fusion | flops 262144 | bytes 1048576 | tf_op jit(solution)/shard_map/sub | solution.py:403
  84.7 0.0 copy-done
  84.7 0.7 copy.9
Async XLA Ops:
  82.8 1.9 %copy-start = (f32[32,1024]{1,0:T(8,128)S(1)}, f32[32,1024]{1,0:T(8,128)}, u32[]{:S(2)}) copy-start(f32[32,1024]{1,0:T(8,128)} %get-tuple-element.9) | copy-start | bytes 393220
where the time goes:
time: 85.5 us; the launch traced here: 85.4 us
  Pallas kernels  82.1 us (96%)
  other arithmetic  1.93 us (2%)
    pallas_call x1, Pallas kernels, per_device(): pl.pallas_call(functools.partial(kernel, nt, steps), name='ista', out_sha...  82.1 us
    sub x1, other arithmetic, per_device(): return (moved - jnp.clip(moved, -SHRINK, SHRINK), resid)  1.93 us

commit v1 on v0

--- a/solution.py
+++ b/solution.py
@@ -36,9 +36,9 @@
     nt, steps,
     vol, meas, rowb, colb, kidx, vord,
     out, resid,
-    V, mz, raw, H, TFh, TFl, TB, AF, A2, AP, Wh, Wl, S, XF, rb1, rb2, res, R, RX,
-    rs_send, rs1_recv, rs2_recv, ag_send, agx_send, ag_recv, agx_recv,
-    loc_sem, pair_send, pair_recv, raw_sem, fin_loc, fin_send, fin_recv,
+    V, mz, raw, H, TFh, TFl, TB, AF, A2, AP, Wh, Wl, S, XF, rb1, rb2, res1, res2, R, RX,
+    rs_send, rs1_recv, rs2_recv, ag1_send, ag2_send, agx1_send, agx2_send,
+    ag1_recv, ag2_recv, agx1_recv, agx2_recv, loc_sem, pair_send, pair_recv, raw_sem, fin_loc, fin_send, fin_recv,
 ):
     dd, t = lax.axis_index("depth"), lax.axis_index("tile")
     kap, z = dd % 2, dd // 2
@@ -46,9 +46,29 @@
     other = 1 - kap
     partner = (z * 2 + other, t)
     reach = (rowb.shape[0] - 1) // 2
-    edge = jnp.logical_or(
-        jnp.logical_and(kap == 0, z == 3), jnp.logical_and(kap == 1, z == 0)
-    )
+    low2 = 2 * (c + p - 1)
+    own2 = 2 * (c - p)
+    inner = jnp.logical_or(z == 1, z == 2)
+    block2 = 2 * p + z - 1
+    edge1 = z == 3 - 3 * kap
+    edge2 = jnp.logical_and(inner, block2 == 3 - 3 * kap)
+
+    def wrapped(tile):
+        return (tile + 2 * nt) % nt
+
+    def owner2(b, core):
+        return ((1 + b % 2) * 2 + core, wrapped(low2 + 3 * (b // 2)))
+
+    def around():
+        for hx in range(2):
+            for bo in range(4):
+                if hx or bo:
+                    yield (p + hx) % 2, (z + bo) % 4
+
+    def members2():
+        for h in range(2):
+            for bo in range(4):
+                yield wrapped(own2 + 2 - h), h, (z + bo) % 4
 
     def cols(block):
         return pl.ds(pl.multiple_of(block * LANES, LANES), LANES)
@@ -75,8 +95,39 @@
         send(vol.at[:, :, cols(block_of(other, lb))], V.at[lb, mine], pair_send.at[lb], pair_recv.at[lb], partner)
         for lb in range(5)
     ]
-    for cp in gives:
-        cp.start()
+    barrier = pltpu.get_barrier_semaphore()
+
+    def greet(dev):
+        pl.semaphore_signal(barrier, inc=1, device_id=dev, device_id_type=MESH)
+
+    greet(partner)
+    for h, b in around():
+        greet((2 * b + kap, 2 * c + h))
+    for b in range(4):
+        greet(owner2(b, kap))
+    far1, far2 = 3 * kap, 3 * kap
+    for h in range(2):
+        greet((2 * far1 + other, 2 * c + h))
+    greet(owner2(far2, other))
+
+    @pl.when(edge1)
+    def _():
+        for h in range(2):
+            for b in range(4):
+                greet((2 * b + other, 2 * c + h))
+
+    @pl.when(inner)
+    def _():
+        for tile, h, b in members2():
+            greet((2 * b + kap, tile))
+
+    @pl.when(edge2)
+    def _():
+        for tile, h, b in members2():
+            greet((2 * b + other, tile))
+
+    n_greets = 1 + 7 + 4 + 3 + 8 * (edge1.astype(jnp.int32) + inner.astype(jnp.int32) + edge2.astype(jnp.int32))
+
     taps = rowb.shape[0]
     j = lax.broadcasted_iota(jnp.int32, (16, rowb.shape[2]), 0)
     pick = jnp.zeros(j.shape, jnp.int32)
@@ -93,8 +144,7 @@
                 precision=lax.Precision.HIGHEST, preferred_element_type=F32,
             )
     give_raw = send(raw.at[kap], raw.at[kap], raw_sem.at[0], raw_sem.at[1], partner)
-    give_raw.start()
-    give_raw.wait()
+    take_raw = send(raw.at[other], raw.at[other], raw_sem.at[0], raw_sem.at[1], partner)
     q = lax.broadcasted_iota(jnp.int32, (LANES, 640), 0)
     l = lax.broadcasted_iota(jnp.int32, (LANES, 640), 1)
     fwd = jnp.logical_and(l < 256, l == jnp.where(q <= reach, reach - q, 256 + reach - q))
@@ -103,9 +153,11 @@
     )
     row = l - 512 == 2 * reach - q
     place = jnp.where(fwd | row, 1.0, jnp.where(bwd, -DESCENT, 0.0)).astype(F32)
-    H[...] = jnp.dot(
-        raw[...].reshape(-1, LANES), place, precision=lax.Precision.HIGHEST, preferred_element_type=F32
-    ).reshape(H.shape)
+
+    def place_taps(core):
+        H[core] = jnp.dot(
+            raw[core].reshape(-1, LANES), place, precision=lax.Precision.HIGHEST, preferred_element_type=F32
+        ).reshape(H.shape[1:])
 
     lane32 = lane_of((32, LANES))
     low = lane32 < 64
@@ -124,8 +176,9 @@
             m = jnp.where(jnp.logical_and(t == nt - 1, lane32 >= 3 * reach), 0.0, m)
             yield r, m
 
-    def prep_forward(k):
-        def plane(d, carry):
+    def prep_forward(k, core):
+        def plane(j, carry):
+            d = core * 4 + j
             base = k * 4 + d % 4
             for r in range(2):
                 hi, lo = split(sheared(taps_of(d // 4, 2 + r, base, 0, 256), LANES))
@@ -138,12 +191,12 @@
                 AF[d, r * 32 : (r + 1) * 32, :] = m
             return carry
 
-        lax.fori_loop(0, 8, plane, 0)
-        for j in range(4):
-            m = AF[2 * j : 2 * j + 2].reshape(LANES, LANES).T[0:64]
+        lax.fori_loop(0, 4, plane, 0)
+        for j in range(2):
+            m = AF[pl.ds(core * 4 + 2 * j, 2)].reshape(LANES, LANES).T[0:64]
             hi, lo = split(m)
-            A2[0:64, j * LANES : (j + 1) * LANES] = hi
-            A2[64:128, j * LANES : (j + 1) * LANES] = lo
+            A2[0:64, cols(core * 2 + j)] = hi
+            A2[64:128, cols(core * 2 + j)] = lo
 
     def prep_backward(k):
         def plane(d, carry):
@@ -164,8 +217,9 @@
 
         lax.fori_loop(0, 8, plane, 0)
 
-    def forward():
-        def plane(d, carry):
+    def forward_planes(core):
+        def plane(j, carry):
+            d = core * 4 + j
             v = [V[lb, d] for lb in range(5)]
             rows = []
             for lb in range(4):
@@ -183,13 +237,15 @@
                     Wl[dst] = lo[src]
             return carry
 
-        lax.fori_loop(0, 8, plane, 0)
+        lax.fori_loop(0, 4, plane, 0)
+
+    def forward_rows():
         s = dot(A2[...], Wh[...].reshape(512, 512))
         s = s[0:64] + s[64:128] + dot(A2[0:64], Wl[...].reshape(512, 512))
         for lb in range(4):
             S[lb] = s[:, lb * 128 : (lb + 1) * 128]
 
-    def backward(k):
+    def backward_rows(k):
         parts = []
         for lb in range(5):
             if lb < 4:
@@ -200,7 +256,9 @@
             parts.append(jnp.concatenate([hi, hi, lo, lo], axis=0))
         XF[...] = dot(AP[...].reshape(512, 256), jnp.concatenate(parts, axis=1)).reshape(8, 64, 640)
 
-        def plane(d, carry):
+    def backward_planes(k, core):
+        def plane(j, carry):
+            d = core * 4 + j
             x = [[XF[d, r * 32 : (r + 1) * 32, lb * 128 : (lb + 1) * 128] for r in range(2)] for lb in range(5)]
             rows = []
             for lb in range(5):
@@ -216,127 +274,185 @@
                 V[lb, d] = new if lb < 4 else jnp.where(keep, new, 0.0)
             return carry
 
-        lax.fori_loop(0, 8, plane, 0)
+        lax.fori_loop(0, 4, plane, 0)
+
+    def rows16(g):
+        return pl.ds(pl.multiple_of(g * 16, 16), 16)
+
+    slot = p * 4 + z
+    half1 = pl.ds(pl.multiple_of((1 - p) * 32, 32), 32)
+    half2 = pl.ds(pl.multiple_of(p * 32, 32), 32)
+    own = rows16(2 - p)
 
     def rs_copies():
-        slot = p * 4 + z
         n = 0
-        cl = c + p - 1
-        for hx in range(2):
-            for bo in range(4):
-                h, b = (p + hx) % 2, (z + bo) % 4
-                if hx or bo:
-                    rows = pl.ds(pl.multiple_of(((1 - p) * 2 + h) * 16, 16), 16)
-                    yield send(S.at[b, rows], rb1.at[slot], rs_send.at[n], rs1_recv.at[slot], (2 * b + kap, 2 * c + h))
-                    n += 1
+        for b in range(4):
+            yield send(S.at[b, half2], rb2.at[slot], rs_send.at[n], rs2_recv.at[slot], owner2(b, kap))
+            n += 1
+        for h, b in around():
+            src = S.at[b, rows16((1 - p) * 2 + h)]
+            yield send(src, rb1.at[slot], rs_send.at[n], rs1_recv.at[slot], (2 * b + kap, 2 * c + h))
+            n += 1
+
+    def ag1_copies():
+        for n, (h, b) in enumerate(around()):
+            g = (1 - h) * 2 + p
+            yield send(res1, R.at[z, rows16(g)], ag1_send.at[n], ag1_recv.at[p, z], (2 * b + kap, 2 * c + h))
+
+    def agx1_copies(k):
         for h in range(2):
-            for bo in range(4):
-                b = (z + bo) % 4
-                rows = pl.ds(pl.multiple_of((2 * p + h) * 16, 16), 16)
-                tile = (2 * cl + 3 * h + nt) % nt
-                yield send(S.at[b, rows], rb2.at[slot], rs_send.at[n], rs2_recv.at[slot], (2 * b + kap, tile))
-                n += 1
-
-    def rs_wait():
-        for hx in range(2):
-            for bo in range(4):
-                slot = ((p + hx) % 2) * 4 + (z + bo) % 4
-                if hx or bo:
-                    send(res.at[0], rb1.at[slot], rs_send.at[0], rs1_recv.at[slot], partner).wait_recv()
-                send(res.at[0], rb2.at[slot], rs_send.at[0], rs2_recv.at[slot], partner).wait_recv()
-
-    def ag_copies(k, far):
-        n = 0
-        core = other if far else kap
-        cl = c - p
-        for kind in range(2):
-            for hx in range(2):
-                for bo in range(4):
-                    h, b = (p + hx) % 2, (z + bo) % 4
-                    if kind == 0:
-                        tile, g = 2 * c + h, (1 - h) * 2 + p
-                        if not (hx or bo or far):
-                            continue
-                    else:
-                        tile, g = (2 * cl + 2 - h + nt) % nt, 2 * h + p
-                    rows = pl.ds(pl.multiple_of(g * 16, 16), 16)
-                    dev = (2 * b + core, tile)
-                    if far:
-                        yield send(res.at[kind], RX.at[k, rows], agx_send.at[n], agx_recv.at[k, g], dev)
-                    else:
-                        yield send(res.at[kind], R.at[z, rows], ag_send.at[n], ag_recv.at[g, z], dev)
-                    n += 1
-
-    def ag_wait(k):
-        for g in range(4):
             for b in range(4):
-                @pl.when(jnp.logical_or(g != 2 - p, b != z))
-                def _():
-                    send(res.at[0], R.at[b, g * 16 : g * 16 + 16], ag_send.at[0], ag_recv.at[g, b], partner).wait_recv()
-            send(res.at[0], RX.at[k, g * 16 : g * 16 + 16], ag_send.at[0], agx_recv.at[k, g], partner).wait_recv()
-
-    prep_forward(0)
+                g = (1 - h) * 2 + p
+                n = h * 4 + b
+                yield send(res1, RX.at[k, rows16(g)], agx1_send.at[n], agx1_recv.at[k, p], (2 * b + other, 2 * c + h))
+
+    def ag2_copies():
+        for n, (tile, h, b) in enumerate(members2()):
+            dst = R.at[block2, pl.ds(pl.multiple_of(h * 32, 32), 32)]
+            yield send(res2, dst, ag2_send.at[n], ag2_recv.at[block2], (2 * b + kap, tile))
+
+    def agx2_copies(k):
+        for n, (tile, h, b) in enumerate(members2()):
+            dst = RX.at[k, pl.ds(pl.multiple_of(h * 32, 32), 32)]
+            yield send(res2, dst, agx2_send.at[n], agx2_recv.at[k], (2 * b + other, tile))
+
+    def came(dst, sem):
+        send(dst, dst, rs_send.at[0], sem, partner).wait_recv()
+
+    def masked_edge(core):
+        for j in range(4):
+            V[4, core * 4 + j] = jnp.where(keep, V[4, core * 4 + j], 0.0)
+
+    place_taps(kap)
+    prep_forward(0, kap)
     for cp in loads:
         cp.wait()
+    masked_edge(kap)
+    pl.semaphore_wait(barrier, n_greets)
+    give_raw.start()
     for cp in gives:
-        cp.wait()
-    for d in range(8):
-        V[4, d] = jnp.where(keep, V[4, d], 0.0)
+        cp.start()
+    forward_planes(kap)
+    take_raw.wait_recv()
+    place_taps(other)
+    prep_forward(0, other)
+    for lb in range(5):
+        came(V.at[lb, theirs], pair_recv.at[lb])
+    masked_edge(other)
+    forward_planes(other)
+    forward_rows()
+    give_raw.wait_send()
+    for cp in gives:
+        cp.wait_send()
+
+    def finals():
+        for lb in range(4):
+            here = cols(kap * 4 + lb)
+            yield send(V.at[lb, theirs], out.at[:, :, here], fin_send.at[lb], fin_recv.at[lb], partner)
+
+    def finals_resid():
+        for lb in range(4):
+            here = cols(kap * 4 + lb)
+            yield send(R.at[lb, 16:48], resid.at[:, here], fin_send.at[4 + lb], fin_recv.at[4 + lb], partner)
+            yield pltpu.make_async_copy(R.at[lb, 16:48], resid.at[:, here], fin_loc.at[4 + lb])
+
+    def finals_here():
+        for lb in range(4):
+            yield pltpu.make_async_copy(V.at[lb, mine], out.at[:, :, cols(kap * 4 + lb)], fin_loc.at[lb])
 
     def step(k, carry):
-        forward()
         S[z, 16:48] = S[z, 16:48] - mz[k]
         for cp in rs_copies():
             cp.start()
         prep_backward(k)
-        rs_wait()
-        own = pl.ds(pl.multiple_of((2 - p) * 16, 16), 16)
-        total1 = S[z, own]
-        total2 = rb2[p * 4 + z]
-        for hx in range(2):
-            for bo in range(4):
-                if hx or bo:
-                    slot = ((p + hx) % 2) * 4 + (z + bo) % 4
-                    total1 = total1 + rb1[slot]
-                    total2 = total2 + rb2[slot]
-        res[0] = total1
-        res[1] = total2
-        for cp in ag_copies(k, False):
+
+        @pl.when(inner)
+        def _():
+            total = jnp.zeros((32, LANES), F32)
+            for q in range(8):
+                came(rb2.at[q], rs2_recv.at[q])
+                total = total + rb2[q]
+            res2[...] = total
+            for cp in ag2_copies():
+                cp.start()
+
+        @pl.when(edge2)
+        def _():
+            for cp in agx2_copies(k):
+                cp.start()
+
+        total = S[z, own]
+        for h, b in around():
+            came(rb1.at[h * 4 + b], rs1_recv.at[h * 4 + b])
+            total = total + rb1[h * 4 + b]
+        res1[...] = total
+        for cp in ag1_copies():
             cp.start()
 
-        @pl.when(edge)
-        def _():
-            for cp in ag_copies(k, True):
+        @pl.when(edge1)
+        def _():
+            for cp in agx1_copies(k):
                 cp.start()
 
-        R[z, own] = total1
-        prep_forward(jnp.minimum(k + 1, steps - 1))
+        R[z, own] = total
+        nxt = jnp.minimum(k + 1, steps - 1)
+        prep_forward(nxt, kap)
+        prep_forward(nxt, other)
         for cp in rs_copies():
             cp.wait_send()
-        ag_wait(k)
-        backward(k)
-        for cp in ag_copies(k, False):
+        for h, b in around():
+            came(R.at[b, rows16((1 - p) * 2 + h)], ag1_recv.at[h, b])
+        for b in range(4):
+            came(R.at[b, half2], ag2_recv.at[b])
+        for h in range(2):
+            came(RX.at[k, rows16((1 - p) * 2 + h)], agx1_recv.at[k, h])
+        came(RX.at[k, half2], agx2_recv.at[k])
+        last = k == steps - 1
+
+        @pl.when(last)
+        def _():
+            for cp in finals_resid():
+                cp.start()
+
+        backward_rows(k)
+        backward_planes(k, other)
+
+        @pl.when(last)
+        def _():
+            for cp in finals():
+                cp.start()
+
+        backward_planes(k, kap)
+        for cp in ag1_copies():
             cp.wait_send()
 
-        @pl.when(edge)
-        def _():
-            for cp in ag_copies(k, True):
+        @pl.when(edge1)
+        def _():
+            for cp in agx1_copies(k):
                 cp.wait_send()
 
+        @pl.when(inner)
+        def _():
+            for cp in ag2_copies():
+                cp.wait_send()
+
+        @pl.when(edge2)
+        def _():
+            for cp in agx2_copies(k):
+                cp.wait_send()
+
+        @pl.when(jnp.logical_not(last))
+        def _():
+            forward_planes(kap)
+            forward_planes(other)
+            forward_rows()
+
         return carry
 
     lax.fori_loop(0, steps, step, 0)
-
-    ends = []
-    for lb in range(4):
-        here = cols(kap * 4 + lb)
-        ends.append(pltpu.make_async_copy(V.at[lb, mine], out.at[:, :, here], fin_loc.at[lb]))
-        ends.append(pltpu.make_async_copy(R.at[lb, 16:48], resid.at[:, here], fin_loc.at[4 + lb]))
-        ends.append(send(V.at[lb, theirs], out.at[:, :, here], fin_send.at[lb], fin_recv.at[lb], partner))
-        ends.append(send(R.at[lb, 16:48], resid.at[:, here], fin_send.at[4 + lb], fin_recv.at[4 + lb], partner))
-    for cp in ends:
+    for cp in finals_here():
         cp.start()
-    for cp in ends:
+    for cp in (*finals_here(), *finals_resid(), *finals()):
         cp.wait()
 
 
@@ -355,8 +471,8 @@
                 jax.ShapeDtypeStruct((rows, width), F32),
             ),
             in_specs=[
-                anywhere,
-                anywhere,
+                pl.BlockSpec(memory_space=pltpu.HBM),
+                pl.BlockSpec(memory_space=pltpu.HBM),
                 pl.BlockSpec(memory_space=vm),
                 pl.BlockSpec(memory_space=vm),
                 pl.BlockSpec(memory_space=pltpu.SMEM),
@@ -379,17 +495,22 @@
                 vm((4, 64, LANES), F32),
                 vm((8, 64, 640), F32),
                 vm((8, 16, LANES), F32),
-                vm((8, 16, LANES), F32),
-                vm((2, 16, LANES), F32),
+                vm((8, 32, LANES), F32),
+                vm((16, LANES), F32),
+                vm((32, LANES), F32),
                 vm((4, 64, LANES), F32),
                 vm((steps, 64, LANES), F32),
-                dma((15,)),
-                dma((8,)),
-                dma((8,)),
-                dma((15,)),
-                dma((16,)),
-                dma((4, 4)),
-                dma((steps, 4)),
+                dma((11,)),
+                dma((8,)),
+                dma((8,)),
+                dma((7,)),
+                dma((8,)),
+                dma((8,)),
+                dma((8,)),
+                dma((2, 4)),
+                dma((4,)),
+                dma((steps, 2)),
+                dma((steps,)),
                 dma((6,)),
                 dma((5,)),
                 dma((5,)),
@@ -398,7 +519,9 @@
                 dma((8,)),
                 dma((8,)),
             ],
-            compiler_params=pltpu.CompilerParams(has_side_effects=True, vmem_limit_bytes=60 * 1024 * 1024),
+            compiler_params=pltpu.CompilerParams(
+                collective_id=0, has_side_effects=True, vmem_limit_bytes=60 * 1024 * 1024
+            ),
         )(volume, measured, row_bank.T, col_bank.T, kernel_index.T, view_order)
         return moved - jnp.clip(moved, -SHRINK, SHRINK), resid
 

time: 85.5 us -> 68.6 us (0.80)
  Pallas kernels: 82.1 us -> 65.2 us
    pallas_call x1, Pallas kernels: 82.1 us -> 65.2 us  [per_device(): pl.pallas_call(functools.partial(kernel, nt, steps), name='ista', out_sha...]
where the time goes in v1:
time: 68.6 us; the launch traced here: 68.4 us
  Pallas kernels  65.2 us (95%)
  other arithmetic  1.93 us (3%)
    pallas_call x1, Pallas kernels, per_device(): pl.pallas_call(functools.partial(kernel, nt, steps), name='ista', out_sha...  65.2 us
    sub x1, other arithmetic, per_device(): return (moved - jnp.clip(moved, -SHRINK, SHRINK), resid)  1.93 us

profile of v1, /device:TPU:1, one launch (start us, length us, event | category | flops | bytes accessed | tf_op | source)
XLA Modules:
  0.0 68.4 jit_solution(8232033372875672831)
XLA Ops:
  0.6 65.2 %ista.1 = (f32[4,32,1024]{2,1,0:T(8,128)}, f32[32,1024]{1,0:T(8,128)}) custom-call(f32[4,32,1024]{2,1,0:T(8,128)} %vol.1, f32[3,32,1024]{2,1,0:T(8,128)} %meas.1, f32[33,2,256]{2,1,0:T(2,128)} %bitcast.3, f32[33,2,256]{2,1,0:T(2,128)} %bitcast.4, s32[4,169]{1,0:T(4,128)} %bitcast.5, s32[3]{0:T(128)} %vord.1), custom_call_target="tpu_custom_call" | custom-call | tf_op jit(solution)/shard_map/ista/pallas_call | solution.py:466
  65.8 0.0 copy-start
  65.8 1.9 %clamp_subtract_fusion = f32[4,32,1024]{2,1,0:T(8,128)} fusion(f32[4,32,1024]{2,1,0:T(8,128)} %get-tuple-element.4), kind=kLoop, calls=%fused_computation | loop fusion | flops 262144 | bytes 1048576 | tf_op jit(solution)/shard_map/sub | solution.py:526
  67.7 0.0 copy-done
  67.8 0.7 copy.9
Async XLA Ops:
  65.8 1.9 %copy-start = (f32[32,1024]{1,0:T(8,128)S(1)}, f32[32,1024]{1,0:T(8,128)}, u32[]{:S(2)}) copy-start(f32[32,1024]{1,0:T(8,128)} %get-tuple-element.9) | copy-start | bytes 393220

commit v2 on v1

--- a/solution.py
+++ b/solution.py
@@ -36,7 +36,7 @@
     nt, steps,
     vol, meas, rowb, colb, kidx, vord,
     out, resid,
-    V, mz, raw, H, TFh, TFl, TB, AF, A2, AP, Wh, Wl, S, XF, rb1, rb2, res1, res2, R, RX,
+    V, mz, raw, H, TFh, TFl, TB, AF, A2, AP, Wh, Wl, S, XF, rb1, rb2, res1, res2, ex1, ex2, R, px1, px2,
     rs_send, rs1_recv, rs2_recv, ag1_send, ag2_send, agx1_send, agx2_send,
     ag1_recv, ag2_recv, agx1_recv, agx2_recv, loc_sem, pair_send, pair_recv, raw_sem, fin_loc, fin_send, fin_recv,
 ):
@@ -60,14 +60,15 @@
         return ((1 + b % 2) * 2 + core, wrapped(low2 + 3 * (b // 2)))
 
     def around():
-        for hx in range(2):
-            for bo in range(4):
+        for hx in (1, 0):
+            for bo in (2, 1, 3, 0):
                 if hx or bo:
                     yield (p + hx) % 2, (z + bo) % 4
 
     def members2():
-        for h in range(2):
-            for bo in range(4):
+        for bo in (2, 3, 1, 0):
+            for hx in (1, 0):
+                h = (p + hx) % 2
                 yield wrapped(own2 + 2 - h), h, (z + bo) % 4
 
     def cols(block):
@@ -191,7 +192,7 @@
                 AF[d, r * 32 : (r + 1) * 32, :] = m
             return carry
 
-        lax.fori_loop(0, 4, plane, 0)
+        lax.fori_loop(0, 4, plane, 0, unroll=True)
         for j in range(2):
             m = AF[pl.ds(core * 4 + 2 * j, 2)].reshape(LANES, LANES).T[0:64]
             hi, lo = split(m)
@@ -220,12 +221,17 @@
     def forward_planes(core):
         def plane(j, carry):
             d = core * 4 + j
-            v = [V[lb, d] for lb in range(5)]
-            rows = []
-            for lb in range(4):
-                near = jnp.where(low, v[lb + 1], v[(lb + 4) % 5])
-                rows.append(jnp.concatenate([v[lb], near], axis=1))
-            hi, lo = split(jnp.concatenate(rows, axis=0))
+            v = [split(V[lb, d]) for lb in range(5)]
+            hi, lo = (
+                jnp.concatenate(
+                    [
+                        jnp.concatenate([v[lb][i], jnp.where(low, v[lb + 1][i], v[(lb + 4) % 5][i])], axis=1)
+                        for lb in range(4)
+                    ],
+                    axis=0,
+                )
+                for i in range(2)
+            )
             w = dot(jnp.concatenate([hi, lo], axis=0), TFh[d])
             w = w[0:128] + w[128:256] + dot(hi, TFl[d])
             hi, lo = split(w)
@@ -237,35 +243,53 @@
                     Wl[dst] = lo[src]
             return carry
 
-        lax.fori_loop(0, 4, plane, 0)
-
-    def forward_rows():
-        s = dot(A2[...], Wh[...].reshape(512, 512))
-        s = s[0:64] + s[64:128] + dot(A2[0:64], Wl[...].reshape(512, 512))
-        for lb in range(4):
-            S[lb] = s[:, lb * 128 : (lb + 1) * 128]
+        lax.fori_loop(0, 4, plane, 0, unroll=True)
+
+    def forward_rows(k):
+        for pair in range(2):
+            at = slice(pair * 256, (pair + 1) * 256)
+            s = dot(A2[...], Wh[:, :, at].reshape(512, 256))
+            s = s[0:64] + s[64:128] + dot(A2[0:64], Wl[:, :, at].reshape(512, 256))
+            for i in range(2):
+                b = 2 * pair + i
+                block = s[:, i * 128 : (i + 1) * 128]
+                S[b, 0:16] = block[0:16]
+                S[b, 16:48] = block[16:48] - jnp.where(z == b, mz[k], 0.0)
+                S[b, 48:64] = block[48:64]
+            for i in range(2):
+                for cp in rs_copies(2 * pair + i):
+                    cp("start")
 
     def backward_rows(k):
-        parts = []
-        for lb in range(5):
-            if lb < 4:
-                r = R[lb]
-            else:
-                r = jnp.where((lane_of((64, LANES)) < 64) == (kap == 0), RX[k], 0.0)
-            hi, lo = split(r)
-            parts.append(jnp.concatenate([hi, hi, lo, lo], axis=0))
-        XF[...] = dot(AP[...].reshape(512, 256), jnp.concatenate(parts, axis=1)).reshape(8, 64, 640)
+        ap = AP[...].reshape(512, 256)
+        for pair in range(3):
+            parts = []
+            for lb in range(2 * pair, min(2 * pair + 2, 5)):
+                if lb < 4:
+                    ag_arrived(lb)
+                    r = R[lb]
+                else:
+                    r = edge_rows(k)
+                hi, lo = split(r)
+                parts.append(jnp.concatenate([hi, hi, lo, lo], axis=0))
+            x = dot(ap, jnp.concatenate(parts, axis=1)).reshape(8, 64, 128 * len(parts))
+            hi, lo = split(x)
+            at = slice(pair * 256, pair * 256 + 128 * len(parts))
+            XF[0, :, :, at] = hi
+            XF[1, :, :, at] = lo
 
     def backward_planes(k, core):
         def plane(j, carry):
             d = core * 4 + j
-            x = [[XF[d, r * 32 : (r + 1) * 32, lb * 128 : (lb + 1) * 128] for r in range(2)] for lb in range(5)]
             rows = []
-            for lb in range(5):
-                near = [jnp.where(low, x[(lb + 1) % 5][r], x[(lb + 4) % 5][r]) for r in range(2)]
-                rows.append(jnp.concatenate(x[lb] + near, axis=1))
-            hi, lo = split(jnp.concatenate(rows, axis=0))
-            g = dot(jnp.concatenate([hi, lo], axis=0), TB[d])
+            for i in range(2):
+                x = [
+                    [XF[i, d, r * 32 : (r + 1) * 32, lb * 128 : (lb + 1) * 128] for r in range(2)] for lb in range(5)
+                ]
+                for lb in range(5):
+                    near = [jnp.where(low, x[(lb + 1) % 5][r], x[(lb + 4) % 5][r]) for r in range(2)]
+                    rows.append(jnp.concatenate(x[lb] + near, axis=1))
+            g = dot(jnp.concatenate(rows, axis=0), TB[d])
             g = g[0:160, 0:128] + (g[0:160, 128:256] + (g[160:320, 0:128] + g[160:320, 128:256]))
             for lb in range(5):
                 moved = V[lb, d] + g[lb * 32 : (lb + 1) * 32]
@@ -274,7 +298,7 @@
                 V[lb, d] = new if lb < 4 else jnp.where(keep, new, 0.0)
             return carry
 
-        lax.fori_loop(0, 4, plane, 0)
+        lax.fori_loop(0, 4, plane, 0, unroll=True)
 
     def rows16(g):
         return pl.ds(pl.multiple_of(g * 16, 16), 16)
@@ -284,15 +308,55 @@
     half2 = pl.ds(pl.multiple_of(p * 32, 32), 32)
     own = rows16(2 - p)
 
-    def rs_copies():
-        n = 0
-        for b in range(4):
-            yield send(S.at[b, half2], rb2.at[slot], rs_send.at[n], rs2_recv.at[slot], owner2(b, kap))
-            n += 1
-        for h, b in around():
+    def guarded(copy, ok):
+        def run(verb):
+            if ok is None:
+                getattr(copy, verb)()
+            else:
+                @pl.when(ok)
+                def _():
+                    getattr(copy, verb)()
+
+        return run
+
+    def rs_copies(b):
+        yield guarded(send(S.at[b, half2], rb2.at[slot], rs_send.at[b], rs2_recv.at[slot], owner2(b, kap)), None)
+        for hx in (1, 0):
+            h = (p + hx) % 2
             src = S.at[b, rows16((1 - p) * 2 + h)]
-            yield send(src, rb1.at[slot], rs_send.at[n], rs1_recv.at[slot], (2 * b + kap, 2 * c + h))
-            n += 1
+            copy = send(src, rb1.at[slot], rs_send.at[4 + hx * 4 + b], rs1_recv.at[slot], (2 * b + kap, 2 * c + h))
+            yield guarded(copy, None if hx else z != b)
+
+    def ag_arrived(b):
+        came(R.at[b, half2], ag2_recv.at[b])
+        for hx in range(2):
+            h = (p + hx) % 2
+            dst = R.at[b, rows16((1 - p) * 2 + h)]
+            guarded(send(dst, dst, rs_send.at[0], ag1_recv.at[h, b], partner), None if hx else z != b)("wait_recv")
+
+    lane8 = lane_of((8, LANES))
+
+    def packed(total):
+        x = jnp.where(kap == 0, pltpu.roll(total, 32, 1), total)
+        y = x[0:8]
+        for i in range(1, total.shape[0] // 8):
+            y = jnp.where(lane8 < 32 * i, y, pltpu.roll(x[8 * i : 8 * i + 8], 32 * i, 1))
+        return y
+
+    def unpacked(y, rows):
+        x = jnp.concatenate([pltpu.roll(y, (128 - 32 * i) % 128, 1) if i else y for i in range(rows // 8)], axis=0)
+        lane = lane_of(x.shape)
+        return jnp.where(
+            kap == 0, jnp.where(lane < 32, x, 0.0), jnp.where(lane >= 96, pltpu.roll(x, 96, 1), 0.0)
+        )
+
+    def edge_rows(k):
+        for h in range(2):
+            came(px1.at[k, h], agx1_recv.at[k, h])
+        came(px2.at[k], agx2_recv.at[k])
+        one = jnp.concatenate([unpacked(px1[k, 0], 16), unpacked(px1[k, 1], 16)], axis=0)
+        two = unpacked(px2[k], 32)
+        return jnp.concatenate([jnp.where(p == 0, two, one), jnp.where(p == 0, one, two)], axis=0)
 
     def ag1_copies():
         for n, (h, b) in enumerate(around()):
@@ -302,9 +366,8 @@
     def agx1_copies(k):
         for h in range(2):
             for b in range(4):
-                g = (1 - h) * 2 + p
                 n = h * 4 + b
-                yield send(res1, RX.at[k, rows16(g)], agx1_send.at[n], agx1_recv.at[k, p], (2 * b + other, 2 * c + h))
+                yield send(ex1, px1.at[k, p], agx1_send.at[n], agx1_recv.at[k, p], (2 * b + other, 2 * c + h))
 
     def ag2_copies():
         for n, (tile, h, b) in enumerate(members2()):
@@ -313,8 +376,7 @@
 
     def agx2_copies(k):
         for n, (tile, h, b) in enumerate(members2()):
-            dst = RX.at[k, pl.ds(pl.multiple_of(h * 32, 32), 32)]
-            yield send(res2, dst, agx2_send.at[n], agx2_recv.at[k], (2 * b + other, tile))
+            yield send(ex2, px2.at[k], agx2_send.at[n], agx2_recv.at[k], (2 * b + other, tile))
 
     def came(dst, sem):
         send(dst, dst, rs_send.at[0], sem, partner).wait_recv()
@@ -340,7 +402,7 @@
         came(V.at[lb, theirs], pair_recv.at[lb])
     masked_edge(other)
     forward_planes(other)
-    forward_rows()
+    forward_rows(0)
     give_raw.wait_send()
     for cp in gives:
         cp.wait_send()
@@ -361,9 +423,6 @@
             yield pltpu.make_async_copy(V.at[lb, mine], out.at[:, :, cols(kap * 4 + lb)], fin_loc.at[lb])
 
     def step(k, carry):
-        S[z, 16:48] = S[z, 16:48] - mz[k]
-        for cp in rs_copies():
-            cp.start()
         prep_backward(k)
 
         @pl.when(inner)
@@ -378,6 +437,7 @@
 
         @pl.when(edge2)
         def _():
+            ex2[...] = packed(res2[...])
             for cp in agx2_copies(k):
                 cp.start()
 
@@ -391,6 +451,7 @@
 
         @pl.when(edge1)
         def _():
+            ex1[...] = packed(total)
             for cp in agx1_copies(k):
                 cp.start()
 
@@ -398,23 +459,18 @@
         nxt = jnp.minimum(k + 1, steps - 1)
         prep_forward(nxt, kap)
         prep_forward(nxt, other)
-        for cp in rs_copies():
-            cp.wait_send()
-        for h, b in around():
-            came(R.at[b, rows16((1 - p) * 2 + h)], ag1_recv.at[h, b])
         for b in range(4):
-            came(R.at[b, half2], ag2_recv.at[b])
-        for h in range(2):
-            came(RX.at[k, rows16((1 - p) * 2 + h)], agx1_recv.at[k, h])
-        came(RX.at[k, half2], agx2_recv.at[k])
+            for cp in rs_copies(b):
+                cp("wait_send")
         last = k == steps - 1
+
+        backward_rows(k)
 
         @pl.when(last)
         def _():
             for cp in finals_resid():
                 cp.start()
 
-        backward_rows(k)
         backward_planes(k, other)
 
         @pl.when(last)
@@ -445,7 +501,7 @@
         def _():
             forward_planes(kap)
             forward_planes(other)
-            forward_rows()
+            forward_rows(k + 1)
 
         return carry
 
@@ -466,10 +522,7 @@
         moved, resid = pl.pallas_call(
             functools.partial(kernel, nt, steps),
             name="ista",
-            out_shape=(
-                jax.ShapeDtypeStruct(volume.shape, F32),
-                jax.ShapeDtypeStruct((rows, width), F32),
-            ),
+            out_shape=(vm(volume.shape, F32), vm((rows, width), F32)),
             in_specs=[
                 pl.BlockSpec(memory_space=pltpu.HBM),
                 pl.BlockSpec(memory_space=pltpu.HBM),
@@ -493,14 +546,17 @@
                 vm((8, 64, 512), BF16),
                 vm((8, 64, 512), BF16),
                 vm((4, 64, LANES), F32),
-                vm((8, 64, 640), F32),
+                vm((2, 8, 64, 640), BF16),
                 vm((8, 16, LANES), F32),
                 vm((8, 32, LANES), F32),
                 vm((16, LANES), F32),
                 vm((32, LANES), F32),
+                vm((8, LANES), F32),
+                vm((8, LANES), F32),
                 vm((4, 64, LANES), F32),
-                vm((steps, 64, LANES), F32),
-                dma((11,)),
+                vm((steps, 2, 8, LANES), F32),
+                vm((steps, 8, LANES), F32),
+                dma((12,)),
                 dma((8,)),
                 dma((8,)),
                 dma((7,)),
@@ -520,7 +576,7 @@
                 dma((8,)),
             ],
             compiler_params=pltpu.CompilerParams(
-                collective_id=0, has_side_effects=True, vmem_limit_bytes=60 * 1024 * 1024
+                collective_id=0, has_side_effects=True, vmem_limit_bytes=61000 << 10
             ),
         )(volume, measured, row_bank.T, col_bank.T, kernel_index.T, view_order)
         return moved - jnp.clip(moved, -SHRINK, SHRINK), resid

time: 68.6 us -> 62.2 us (0.907)
  Pallas kernels: 65.2 us -> 59.9 us
  other arithmetic: 1.93 us -> 0.85 us
    pallas_call x1, Pallas kernels: 65.2 us -> 59.9 us  [per_device(): pl.pallas_call(functools.partial(kernel, nt, steps), name='ista', out_sha...]
    sub x1, other arithmetic: 1.93 us -> 0.85 us  [per_device(): return (moved - jnp.clip(moved, -SHRINK, SHRINK), resid)]
where the time goes in v2:
time: 62.2 us; the launch traced here: 62 us
  Pallas kernels  59.9 us (96%)
  other arithmetic  0.85 us (1%)
  local copies, waits for them, and re-layouts  0.65 us (1%)
  between operations  0.64 us (1%)
    pallas_call x1, Pallas kernels, per_device(): pl.pallas_call(functools.partial(kernel, nt, steps), name='ista', out_sha...  59.9 us

profile of v2, /device:TPU:1, one launch (start us, length us, event | category | flops | bytes accessed | tf_op | source)
XLA Modules:
  0.0 62.0 jit_solution(6052651617446148387)
XLA Ops:
  0.6 59.9 %ista.1 = (f32[4,32,1024]{2,1,0:T(8,128)S(1)}, f32[32,1024]{1,0:T(8,128)S(1)}) custom-call(f32[4,32,1024]{2,1,0:T(8,128)} %vol.1, f32[3,32,1024]{2,1,0:T(8,128)} %meas.1, f32[33,2,256]{2,1,0:T(2,128)} %bitcast.3, f32[33,2,256]{2,1,0:T(2,128)} %bitcast.4, s32[4,169]{1,0:T(4,128)} %bitcast.5, s32[3]{0:T(128)} %vord.1), custom_call_target="tpu_custom_call" | custom-call | tf_op jit(solution)/shard_map/ista/pallas_call | solution.py:522
  60.5 0.8 %clamp_subtract_fusion = f32[4,32,1024]{2,1,0:T(8,128)} fusion(f32[4,32,1024]{2,1,0:T(8,128)S(1)} %get-tuple-element.4), kind=kLoop, calls=%fused_computation | loop fusion | flops 262144 | bytes 1048576 | tf_op jit(solution)/shard_map/sub | solution.py:582
  61.4 0.7 %copy.9 = f32[32,1024]{1,0:T(8,128)} copy(f32[32,1024]{1,0:T(8,128)S(1)} %get-tuple-element.7) | data formatting | bytes 262144

commit v3 on v2

--- a/solution.py
+++ b/solution.py
@@ -49,27 +49,29 @@
     low2 = 2 * (c + p - 1)
     own2 = 2 * (c - p)
     inner = jnp.logical_or(z == 1, z == 2)
-    block2 = 2 * p + z - 1
+    pair2 = z - 1
     edge1 = z == 3 - 3 * kap
-    edge2 = jnp.logical_and(inner, block2 == 3 - 3 * kap)
+    edge2 = z == 2 - kap
+    whole_src = jnp.logical_and(t != 0, t != nt - 1)
+    whole_own = jnp.logical_and(t != 1, t != nt - 2)
 
     def wrapped(tile):
         return (tile + 2 * nt) % nt
 
-    def owner2(b, core):
-        return ((1 + b % 2) * 2 + core, wrapped(low2 + 3 * (b // 2)))
-
-    def around():
-        for hx in (1, 0):
-            for bo in (2, 1, 3, 0):
-                if hx or bo:
-                    yield (p + hx) % 2, (z + bo) % 4
-
-    def members2():
-        for bo in (2, 3, 1, 0):
-            for hx in (1, 0):
-                h = (p + hx) % 2
-                yield wrapped(own2 + 2 - h), h, (z + bo) % 4
+    def owner2(h, pair, core):
+        return ((1 + pair) * 2 + core, wrapped(low2 + 3 * h))
+
+    FAR, NEAR = (4, 3, 5), (2, 6, 1, 7)
+
+    def around(offsets=FAR + NEAR):
+        for offset in offsets:
+            place = (4 * p + z + offset) % 8
+            yield place // 4, place % 4
+
+    def members2(offsets=FAR + NEAR + (0,)):
+        for offset in offsets:
+            place = (4 * p + z + offset) % 8
+            yield wrapped(own2 + 2 - place // 4), place // 4, place % 4
 
     def cols(block):
         return pl.ds(pl.multiple_of(block * LANES, LANES), LANES)
@@ -96,6 +98,8 @@
         send(vol.at[:, :, cols(block_of(other, lb))], V.at[lb, mine], pair_send.at[lb], pair_recv.at[lb], partner)
         for lb in range(5)
     ]
+    R[...] = jnp.zeros_like(R)
+    px2[...] = jnp.zeros_like(px2)
     barrier = pltpu.get_barrier_semaphore()
 
     def greet(dev):
@@ -104,12 +108,11 @@
     greet(partner)
     for h, b in around():
         greet((2 * b + kap, 2 * c + h))
-    for b in range(4):
-        greet(owner2(b, kap))
-    far1, far2 = 3 * kap, 3 * kap
     for h in range(2):
-        greet((2 * far1 + other, 2 * c + h))
-    greet(owner2(far2, other))
+        for pair in range(2):
+            greet(owner2(h, pair, kap))
+        greet((2 * (3 * kap) + other, 2 * c + h))
+        greet(owner2(h, kap, other))
 
     @pl.when(edge1)
     def _():
@@ -127,7 +130,7 @@
         for tile, h, b in members2():
             greet((2 * b + other, tile))
 
-    n_greets = 1 + 7 + 4 + 3 + 8 * (edge1.astype(jnp.int32) + inner.astype(jnp.int32) + edge2.astype(jnp.int32))
+    n_greets = 1 + 7 + 4 + 4 + 8 * (edge1.astype(jnp.int32) + inner.astype(jnp.int32) + edge2.astype(jnp.int32))
 
     taps = rowb.shape[0]
     j = lax.broadcasted_iota(jnp.int32, (16, rowb.shape[2]), 0)
@@ -199,8 +202,9 @@
             A2[0:64, cols(core * 2 + j)] = hi
             A2[64:128, cols(core * 2 + j)] = lo
 
-    def prep_backward(k):
-        def plane(d, carry):
+    def prep_backward(k, core):
+        def plane(j, carry):
+            d = core * 4 + j
             base = k * 4 + d % 4
             for r in range(2):
                 hi, lo = split(sheared(taps_of(d // 4, 2 + r, base, 256, 512), LANES))
@@ -216,7 +220,7 @@
                 AP[d, at, 128:256] = hi
             return carry
 
-        lax.fori_loop(0, 8, plane, 0)
+        lax.fori_loop(0, 4, plane, 0, unroll=True)
 
     def forward_planes(core):
         def plane(j, carry):
@@ -256,17 +260,17 @@
                 S[b, 0:16] = block[0:16]
                 S[b, 16:48] = block[16:48] - jnp.where(z == b, mz[k], 0.0)
                 S[b, 48:64] = block[48:64]
-            for i in range(2):
-                for cp in rs_copies(2 * pair + i):
-                    cp("start")
+        for cp in rs_copies(0):
+            cp("start")
 
     def backward_rows(k):
         ap = AP[...].reshape(512, 256)
         for pair in range(3):
             parts = []
+            if pair < 2:
+                ag_arrived(pair)
             for lb in range(2 * pair, min(2 * pair + 2, 5)):
                 if lb < 4:
-                    ag_arrived(lb)
                     r = R[lb]
                 else:
                     r = edge_rows(k)
@@ -304,8 +308,6 @@
         return pl.ds(pl.multiple_of(g * 16, 16), 16)
 
     slot = p * 4 + z
-    half1 = pl.ds(pl.multiple_of((1 - p) * 32, 32), 32)
-    half2 = pl.ds(pl.multiple_of(p * 32, 32), 32)
     own = rows16(2 - p)
 
     def guarded(copy, ok):
@@ -319,20 +321,26 @@
 
         return run
 
-    def rs_copies(b):
-        yield guarded(send(S.at[b, half2], rb2.at[slot], rs_send.at[b], rs2_recv.at[slot], owner2(b, kap)), None)
+    def rs_copies(part):
+        if part == 0:
+            for i in range(4):
+                h, pair = (p if i < 2 else 1 - p), i % 2
+                src = S.at[2 * pair : 2 * pair + 2, rows16(2 * p + h)]
+                copy = send(src, rb2.at[slot], rs_send.at[7 + i], rs2_recv.at[slot], owner2(h, pair, kap))
+                yield guarded(copy, whole_src if i < 2 else None)
+        for n, (h, b) in enumerate(around((FAR, NEAR)[part])):
+            src = S.at[b, rows16((1 - p) * 2 + h)]
+            copy = send(src, rb1.at[slot], rs_send.at[3 * part + n], rs1_recv.at[slot], (2 * b + kap, 2 * c + h))
+            yield guarded(copy, None)
+
+    def ag_arrived(pair):
         for hx in (1, 0):
             h = (p + hx) % 2
-            src = S.at[b, rows16((1 - p) * 2 + h)]
-            copy = send(src, rb1.at[slot], rs_send.at[4 + hx * 4 + b], rs1_recv.at[slot], (2 * b + kap, 2 * c + h))
-            yield guarded(copy, None if hx else z != b)
-
-    def ag_arrived(b):
-        came(R.at[b, half2], ag2_recv.at[b])
-        for hx in range(2):
-            h = (p + hx) % 2
-            dst = R.at[b, rows16((1 - p) * 2 + h)]
-            guarded(send(dst, dst, rs_send.at[0], ag1_recv.at[h, b], partner), None if hx else z != b)("wait_recv")
+            for b in (2 * pair, 2 * pair + 1):
+                dst = R.at[b, rows16((1 - p) * 2 + h)]
+                guarded(send(dst, dst, rs_send.at[0], ag1_recv.at[h, b], partner), None if hx else z != b)("wait_recv")
+            dst = R.at[2 * pair : 2 * pair + 2, rows16(2 * p + h)]
+            guarded(send(dst, dst, rs_send.at[0], ag2_recv.at[h, pair], partner), None if hx else whole_src)("wait_recv")
 
     lane8 = lane_of((8, LANES))
 
@@ -353,15 +361,18 @@
     def edge_rows(k):
         for h in range(2):
             came(px1.at[k, h], agx1_recv.at[k, h])
-        came(px2.at[k], agx2_recv.at[k])
+        for hx in (1, 0):
+            h = (p + hx) % 2
+            dst = px2.at[k, h]
+            guarded(send(dst, dst, rs_send.at[0], agx2_recv.at[k, h], partner), None if hx else whole_src)("wait_recv")
         one = jnp.concatenate([unpacked(px1[k, 0], 16), unpacked(px1[k, 1], 16)], axis=0)
-        two = unpacked(px2[k], 32)
+        two = jnp.concatenate([unpacked(px2[k, 0], 16), unpacked(px2[k, 1], 16)], axis=0)
         return jnp.concatenate([jnp.where(p == 0, two, one), jnp.where(p == 0, one, two)], axis=0)
 
-    def ag1_copies():
-        for n, (h, b) in enumerate(around()):
+    def ag1_copies(part):
+        for n, (h, b) in enumerate(around((FAR, NEAR)[part])):
             g = (1 - h) * 2 + p
-            yield send(res1, R.at[z, rows16(g)], ag1_send.at[n], ag1_recv.at[p, z], (2 * b + kap, 2 * c + h))
+            yield send(res1, R.at[z, rows16(g)], ag1_send.at[3 * part + n], ag1_recv.at[p, z], (2 * b + kap, 2 * c + h))
 
     def agx1_copies(k):
         for h in range(2):
@@ -369,14 +380,16 @@
                 n = h * 4 + b
                 yield send(ex1, px1.at[k, p], agx1_send.at[n], agx1_recv.at[k, p], (2 * b + other, 2 * c + h))
 
-    def ag2_copies():
-        for n, (tile, h, b) in enumerate(members2()):
-            dst = R.at[block2, pl.ds(pl.multiple_of(h * 32, 32), 32)]
-            yield send(res2, dst, ag2_send.at[n], ag2_recv.at[block2], (2 * b + kap, tile))
+    def ag2_copies(part):
+        for n, (tile, h, b) in enumerate(members2((FAR + NEAR[:2], NEAR[2:] + (0,))[part])):
+            dst = R.at[pl.ds(2 * pair2, 2), rows16(2 * h + p)]
+            copy = send(res2, dst, ag2_send.at[5 * part + n], ag2_recv.at[p, pair2], (2 * b + kap, tile))
+            yield guarded(copy, jnp.logical_or(whole_own, h != p))
 
     def agx2_copies(k):
         for n, (tile, h, b) in enumerate(members2()):
-            yield send(ex2, px2.at[k], agx2_send.at[n], agx2_recv.at[k], (2 * b + other, tile))
+            copy = send(ex2, px2.at[k, p], agx2_send.at[n], agx2_recv.at[k, p], (2 * b + other, tile))
+            yield guarded(copy, jnp.logical_or(whole_own, h != p))
 
     def came(dst, sem):
         send(dst, dst, rs_send.at[0], sem, partner).wait_recv()
@@ -423,30 +436,34 @@
             yield pltpu.make_async_copy(V.at[lb, mine], out.at[:, :, cols(kap * 4 + lb)], fin_loc.at[lb])
 
     def step(k, carry):
-        prep_backward(k)
+        for cp in rs_copies(1):
+            cp("start")
+        prep_backward(k, kap)
+        prep_backward(k, other)
 
         @pl.when(inner)
         def _():
-            total = jnp.zeros((32, LANES), F32)
-            for q in range(8):
-                came(rb2.at[q], rs2_recv.at[q])
-                total = total + rb2[q]
+            total = jnp.zeros((2, 16, LANES), F32)
+            for _, h, b in members2():
+                q, ok = h * 4 + b, jnp.logical_or(whole_own, h != p)
+                guarded(send(res2, rb2.at[q], rs_send.at[0], rs2_recv.at[q], partner), ok)("wait_recv")
+                total = total + jnp.where(ok, rb2[q], 0.0)
             res2[...] = total
-            for cp in ag2_copies():
-                cp.start()
+            for cp in ag2_copies(0):
+                cp("start")
 
         @pl.when(edge2)
         def _():
-            ex2[...] = packed(res2[...])
+            ex2[...] = packed(jnp.where(kap == 0, res2[1], res2[0]))
             for cp in agx2_copies(k):
-                cp.start()
+                cp("start")
 
         total = S[z, own]
         for h, b in around():
             came(rb1.at[h * 4 + b], rs1_recv.at[h * 4 + b])
             total = total + rb1[h * 4 + b]
         res1[...] = total
-        for cp in ag1_copies():
+        for cp in ag1_copies(0):
             cp.start()
 
         @pl.when(edge1)
@@ -457,11 +474,18 @@
 
         R[z, own] = total
         nxt = jnp.minimum(k + 1, steps - 1)
+        for cp in ag1_copies(1):
+            cp.start()
+
+        @pl.when(inner)
+        def _():
+            for cp in ag2_copies(1):
+                cp("start")
+
         prep_forward(nxt, kap)
         prep_forward(nxt, other)
-        for b in range(4):
-            for cp in rs_copies(b):
-                cp("wait_send")
+        for cp in (*rs_copies(0), *rs_copies(1)):
+            cp("wait_send")
         last = k == steps - 1
 
         backward_rows(k)
@@ -479,7 +503,7 @@
                 cp.start()
 
         backward_planes(k, kap)
-        for cp in ag1_copies():
+        for cp in (*ag1_copies(0), *ag1_copies(1)):
             cp.wait_send()
 
         @pl.when(edge1)
@@ -489,13 +513,13 @@
 
         @pl.when(inner)
         def _():
-            for cp in ag2_copies():
-                cp.wait_send()
+            for cp in (*ag2_copies(0), *ag2_copies(1)):
+                cp("wait_send")
 
         @pl.when(edge2)
         def _():
             for cp in agx2_copies(k):
-                cp.wait_send()
+                cp("wait_send")
 
         @pl.when(jnp.logical_not(last))
         def _():
@@ -548,15 +572,15 @@
                 vm((4, 64, LANES), F32),
                 vm((2, 8, 64, 640), BF16),
                 vm((8, 16, LANES), F32),
-                vm((8, 32, LANES), F32),
+                vm((8, 2, 16, LANES), F32),
                 vm((16, LANES), F32),
-                vm((32, LANES), F32),
+                vm((2, 16, LANES), F32),
                 vm((8, LANES), F32),
                 vm((8, LANES), F32),
                 vm((4, 64, LANES), F32),
                 vm((steps, 2, 8, LANES), F32),
-                vm((steps, 8, LANES), F32),
-                dma((12,)),
+                vm((steps, 2, 8, LANES), F32),
+                dma((11,)),
                 dma((8,)),
                 dma((8,)),
                 dma((7,)),
@@ -564,9 +588,9 @@
                 dma((8,)),
                 dma((8,)),
                 dma((2, 4)),
-                dma((4,)),
+                dma((2, 2)),
                 dma((steps, 2)),
-                dma((steps,)),
+                dma((steps, 2)),
                 dma((6,)),
                 dma((5,)),
                 dma((5,)),

time: 62.2 us -> 59.5 us (0.957)
  Pallas kernels: 59.9 us -> 57 us
    pallas_call x1, Pallas kernels: 59.9 us -> 57 us  [per_device(): pl.pallas_call(functools.partial(kernel, nt, steps), name='ista', out_sha...]
where the time goes in v3:
time: 59.5 us; the launch traced here: 59.2 us
  Pallas kernels  57 us (96%)
  other arithmetic  0.85 us (1%)
  local copies, waits for them, and re-layouts  0.65 us (1%)
  between operations  0.64 us (1%)
    pallas_call x1, Pallas kernels, per_device(): pl.pallas_call(functools.partial(kernel, nt, steps), name='ista', out_sha...  57 us

profile of v3, /device:TPU:1, one launch (start us, length us, event | category | flops | bytes accessed | tf_op | source)
XLA Modules:
  0.0 59.2 jit_solution(8685664445108717596)
XLA Ops:
  0.6 57.0 %ista.1 = (f32[4,32,1024]{2,1,0:T(8,128)S(1)}, f32[32,1024]{1,0:T(8,128)S(1)}) custom-call(f32[4,32,1024]{2,1,0:T(8,128)} %vol.1, f32[3,32,1024]{2,1,0:T(8,128)} %meas.1, f32[33,2,256]{2,1,0:T(2,128)} %bitcast.3, f32[33,2,256]{2,1,0:T(2,128)} %bitcast.4, s32[4,169]{1,0:T(4,128)} %bitcast.5, s32[3]{0:T(128)} %vord.1), custom_call_target="tpu_custom_call" | custom-call | tf_op jit(solution)/shard_map/ista/pallas_call | solution.py:546
  57.7 0.8 %clamp_subtract_fusion = f32[4,32,1024]{2,1,0:T(8,128)} fusion(f32[4,32,1024]{2,1,0:T(8,128)S(1)} %get-tuple-element.4), kind=kLoop, calls=%fused_computation | loop fusion | flops 262144 | bytes 1048576 | tf_op jit(solution)/shard_map/sub | solution.py:606
  58.5 0.7 %copy.9 = f32[32,1024]{1,0:T(8,128)} copy(f32[32,1024]{1,0:T(8,128)S(1)} %get-tuple-element.7) | data formatting | bytes 262144

commit v4 on v3

--- a/solution.py
+++ b/solution.py
@@ -81,6 +81,40 @@
             src_ref=src, dst_ref=dst, send_sem=s, recv_sem=r, device_id=dev, device_id_type=MESH
         )
 
+    R[...] = jnp.zeros_like(R)
+    px2[...] = jnp.zeros_like(px2)
+    barrier = pltpu.get_barrier_semaphore()
+
+    def greet(dev):
+        pl.semaphore_signal(barrier, inc=1, device_id=dev, device_id_type=MESH)
+
+    for h, b in around():
+        greet((2 * b + kap, 2 * c + h))
+    for h in range(2):
+        for pair in range(2):
+            greet(owner2(h, pair, kap))
+        greet((2 * (3 * kap) + other, 2 * c + h))
+        greet(owner2(h, kap, other))
+
+    @pl.when(edge1)
+    def _():
+        for h in range(2):
+            for b in range(4):
+                greet((2 * b + other, 2 * c + h))
+
+    @pl.when(inner)
+    def _():
+        for tile, h, b in members2():
+            greet((2 * b + kap, tile))
+
+    @pl.when(edge2)
+    def _():
+        for tile, h, b in members2():
+            greet((2 * b + other, tile))
+
+    greet(partner)
+    n_greets = 1 + 7 + 4 + 4 + 8 * (edge1.astype(jnp.int32) + inner.astype(jnp.int32) + edge2.astype(jnp.int32))
+
     mine = pl.ds(kap * 4, 4)
     theirs = pl.ds(other * 4, 4)
 
@@ -98,40 +132,6 @@
         send(vol.at[:, :, cols(block_of(other, lb))], V.at[lb, mine], pair_send.at[lb], pair_recv.at[lb], partner)
         for lb in range(5)
     ]
-    R[...] = jnp.zeros_like(R)
-    px2[...] = jnp.zeros_like(px2)
-    barrier = pltpu.get_barrier_semaphore()
-
-    def greet(dev):
-        pl.semaphore_signal(barrier, inc=1, device_id=dev, device_id_type=MESH)
-
-    greet(partner)
-    for h, b in around():
-        greet((2 * b + kap, 2 * c + h))
-    for h in range(2):
-        for pair in range(2):
-            greet(owner2(h, pair, kap))
-        greet((2 * (3 * kap) + other, 2 * c + h))
-        greet(owner2(h, kap, other))
-
-    @pl.when(edge1)
-    def _():
-        for h in range(2):
-            for b in range(4):
-                greet((2 * b + other, 2 * c + h))
-
-    @pl.when(inner)
-    def _():
-        for tile, h, b in members2():
-            greet((2 * b + kap, tile))
-
-    @pl.when(edge2)
-    def _():
-        for tile, h, b in members2():
-            greet((2 * b + other, tile))
-
-    n_greets = 1 + 7 + 4 + 4 + 8 * (edge1.astype(jnp.int32) + inner.astype(jnp.int32) + edge2.astype(jnp.int32))
-
     taps = rowb.shape[0]
     j = lax.broadcasted_iota(jnp.int32, (16, rowb.shape[2]), 0)
     pick = jnp.zeros(j.shape, jnp.int32)
@@ -381,7 +381,7 @@
                 yield send(ex1, px1.at[k, p], agx1_send.at[n], agx1_recv.at[k, p], (2 * b + other, 2 * c + h))
 
     def ag2_copies(part):
-        for n, (tile, h, b) in enumerate(members2((FAR + NEAR[:2], NEAR[2:] + (0,))[part])):
+        for n, (tile, h, b) in enumerate(members2(((4, 2, 6, 3, 5), (1, 7, 0))[part])):
             dst = R.at[pl.ds(2 * pair2, 2), rows16(2 * h + p)]
             copy = send(res2, dst, ag2_send.at[5 * part + n], ag2_recv.at[p, pair2], (2 * b + kap, tile))
             yield guarded(copy, jnp.logical_or(whole_own, h != p))
@@ -435,11 +435,34 @@
         for lb in range(4):
             yield pltpu.make_async_copy(V.at[lb, mine], out.at[:, :, cols(kap * 4 + lb)], fin_loc.at[lb])
 
+    def ag_sent(k):
+        for cp in (*ag1_copies(0), *ag1_copies(1)):
+            cp.wait_send()
+
+        @pl.when(edge1)
+        def _():
+            for cp in agx1_copies(k):
+                cp.wait_send()
+
+        @pl.when(inner)
+        def _():
+            for cp in (*ag2_copies(0), *ag2_copies(1)):
+                cp("wait_send")
+
+        @pl.when(edge2)
+        def _():
+            for cp in agx2_copies(k):
+                cp("wait_send")
+
     def step(k, carry):
         for cp in rs_copies(1):
             cp("start")
         prep_backward(k, kap)
         prep_backward(k, other)
+
+        @pl.when(k > 0)
+        def _():
+            ag_sent(k - 1)
 
         @pl.when(inner)
         def _():
@@ -449,13 +472,7 @@
                 guarded(send(res2, rb2.at[q], rs_send.at[0], rs2_recv.at[q], partner), ok)("wait_recv")
                 total = total + jnp.where(ok, rb2[q], 0.0)
             res2[...] = total
-            for cp in ag2_copies(0):
-                cp("start")
-
-        @pl.when(edge2)
-        def _():
-            ex2[...] = packed(jnp.where(kap == 0, res2[1], res2[0]))
-            for cp in agx2_copies(k):
+            for cp in (*ag2_copies(0), *ag2_copies(1)):
                 cp("start")
 
         total = S[z, own]
@@ -466,21 +483,22 @@
         for cp in ag1_copies(0):
             cp.start()
 
-        @pl.when(edge1)
-        def _():
-            ex1[...] = packed(total)
-            for cp in agx1_copies(k):
-                cp.start()
-
         R[z, own] = total
         nxt = jnp.minimum(k + 1, steps - 1)
         for cp in ag1_copies(1):
             cp.start()
 
-        @pl.when(inner)
-        def _():
-            for cp in ag2_copies(1):
+        @pl.when(edge2)
+        def _():
+            ex2[...] = packed(jnp.where(kap == 0, res2[1], res2[0]))
+            for cp in agx2_copies(k):
                 cp("start")
+
+        @pl.when(edge1)
+        def _():
+            ex1[...] = packed(total)
+            for cp in agx1_copies(k):
+                cp.start()
 
         prep_forward(nxt, kap)
         prep_forward(nxt, other)
@@ -503,24 +521,6 @@
                 cp.start()
 
         backward_planes(k, kap)
-        for cp in (*ag1_copies(0), *ag1_copies(1)):
-            cp.wait_send()
-
-        @pl.when(edge1)
-        def _():
-            for cp in agx1_copies(k):
-                cp.wait_send()
-
-        @pl.when(inner)
-        def _():
-            for cp in (*ag2_copies(0), *ag2_copies(1)):
-                cp("wait_send")
-
-        @pl.when(edge2)
-        def _():
-            for cp in agx2_copies(k):
-                cp("wait_send")
-
         @pl.when(jnp.logical_not(last))
         def _():
             forward_planes(kap)
@@ -530,6 +530,7 @@
         return carry
 
     lax.fori_loop(0, steps, step, 0)
+    ag_sent(steps - 1)
     for cp in finals_here():
         cp.start()
     for cp in (*finals_here(), *finals_resid(), *finals()):

time: 59.5 us -> 59.7 us (level)
  no operation moved by 1% of the time
where the time goes in v4:
time: 59.7 us; the launch traced here: 59.5 us
  Pallas kernels  57.4 us (96%)
  other arithmetic  0.85 us (1%)
  local copies, waits for them, and re-layouts  0.65 us (1%)
  between operations  0.64 us (1%)
    pallas_call x1, Pallas kernels, per_device(): pl.pallas_call(functools.partial(kernel, nt, steps), name='ista', out_sha...  57.4 us

profile of v4, /device:TPU:1, one launch (start us, length us, event | category | flops | bytes accessed | tf_op | source)
XLA Modules:
  0.0 59.5 jit_solution(3854971960884792728)
XLA Ops:
  0.6 57.4 %ista.1 = (f32[4,32,1024]{2,1,0:T(8,128)S(1)}, f32[32,1024]{1,0:T(8,128)S(1)}) custom-call(f32[4,32,1024]{2,1,0:T(8,128)} %vol.1, f32[3,32,1024]{2,1,0:T(8,128)} %meas.1, f32[33,2,256]{2,1,0:T(2,128)} %bitcast.3, f32[33,2,256]{2,1,0:T(2,128)} %bitcast.4, s32[4,169]{1,0:T(4,128)} %bitcast.5, s32[3]{0:T(128)} %vord.1), custom_call_target="tpu_custom_call" | custom-call | tf_op jit(solution)/shard_map/ista/pallas_call | solution.py:547
  58.0 0.8 %clamp_subtract_fusion = f32[4,32,1024]{2,1,0:T(8,128)} fusion(f32[4,32,1024]{2,1,0:T(8,128)S(1)} %get-tuple-element.4), kind=kLoop, calls=%fused_computation | loop fusion | flops 262144 | bytes 1048576 | tf_op jit(solution)/shard_map/sub | solution.py:607
  58.9 0.7 %copy.9 = f32[32,1024]{1,0:T(8,128)} copy(f32[32,1024]{1,0:T(8,128)S(1)} %get-tuple-element.7) | data formatting | bytes 262144
